TPU v7x, 32 devices: a whole 2x2x4 slice. The times are simulated.
32 devices in a mesh: layer: 16 (over z, y, core), dp: 2 (over x).
Axes of the slice: x: 2, y: 2, z: 4, core: 2. Of those that a mesh axis runs over, the one named last changes fastest.
Arguments:
- c_guess: float32 [16, 256, 512], P('layer', 'dp'), may hold values from -6 to 6
- adj_guess: float32 [16, 256, 512], P('layer', 'dp'), may hold values from -6 to 6
- norm_gain: float32 [32, 512], P('layer'), may hold values from 0.5 to 1.5
- w_up: bfloat16 [32, 512, 2048], P('layer'), may hold values from -0.25 to 0.25
- w_down: bfloat16 [32, 2048, 512], P('layer'), may hold values from -0.125 to 0.125
- coarse_rate: float32 [16, 512], P('layer'), may hold values from 0.5 to 1
Outputs:
- c_points: float32 [16, 256, 512], P('layer', 'dp')
- adj_points: float32 [16, 256, 512], P('layer', 'dp')
- grad_up: float32 [32, 512, 2048], P('layer', 'dp')
- grad_down: float32 [32, 2048, 512], P('layer', 'dp')
All inputs are finite; a program needn't handle non-finite values.
Results may differ from a plain program's by a relative error of at most 0.018.
Values may be sent and summed in bfloat16 or wider, within the bound.
A program may use at most 64 MiB of HBM per device.

v0:
```python
import jax
import jax.numpy as jnp
from jax import lax
from jax.sharding import PartitionSpec as P

eps = 1e-06
step_length = 0.5


def carried_in(x, axis, combine, identity, reverse):
    size, here = (lax.axis_size(axis), lax.axis_index(axis))
    everything = jax.tree.map(lambda part: lax.all_gather(part, axis), x)
    start = jax.tree.map(
        lambda part, zero: jnp.broadcast_to(jnp.asarray(zero, part.dtype), part.shape), x, identity
    )

    def step(k, before):
        at = size - 1 - k if reverse else k
        reached = at > here if reverse else at < here
        new = combine(before, jax.tree.map(lambda part: part[at], everything))
        return jax.tree.map(lambda a, b: jnp.where(reached, a, b), new, before)

    return lax.fori_loop(0, size, step, start)


def normalize(state):
    inverse_rms = lax.rsqrt(jnp.mean(state * state, axis=-1, keepdims=True) + eps)
    return (state * inverse_rms, inverse_rms)


def layer_forward(state, gain_row, up_matrix, down_matrix):
    unit_state, inverse_rms = normalize(state)
    normed = (unit_state * gain_row).astype(jnp.bfloat16)
    preact = jnp.dot(normed, up_matrix, preferred_element_type=jnp.float32)
    hidden = jax.nn.silu(preact).astype(jnp.bfloat16)
    return state + step_length * jnp.dot(hidden, down_matrix, preferred_element_type=jnp.float32)


def layer_backward(state, cotangent, gain_row, up_matrix, down_matrix):
    unit_state, inverse_rms = normalize(state)
    normed = (unit_state * gain_row).astype(jnp.bfloat16)
    preact = jnp.dot(normed, up_matrix, preferred_element_type=jnp.float32)
    hidden = jax.nn.silu(preact).astype(jnp.bfloat16)
    sigmoid_pre = jax.nn.sigmoid(preact)
    out_grad = (step_length * cotangent).astype(jnp.bfloat16)
    hidden_grad = jnp.dot(out_grad, down_matrix.T, preferred_element_type=jnp.float32)
    pre_grad = (hidden_grad * sigmoid_pre * (1.0 + preact * (1.0 - sigmoid_pre))).astype(
        jnp.bfloat16
    )
    normed_grad = jnp.dot(pre_grad, up_matrix.T, preferred_element_type=jnp.float32)
    unit_grad = normed_grad * gain_row
    inner = jnp.mean(unit_grad * unit_state, axis=-1, keepdims=True)
    new_cotangent = cotangent + inverse_rms * (unit_grad - unit_state * inner)
    return (new_cotangent, normed, pre_grad, hidden, out_grad)


def block_forward(state, gains, ups, downs):
    for depth_index in range(gains.shape[0]):
        state = layer_forward(state, gains[depth_index], ups[depth_index], downs[depth_index])
    return state


def block_inputs(state, gains, ups, downs):
    inputs = [state]
    state = layer_forward(state, gains[0], ups[0], downs[0])
    inputs.append(state)
    return inputs


def block_backward(inputs, cotangent, gains, ups, downs):
    normed_list, pre_list, hidden_list, out_list = ([], [], [], [])
    for depth_index in reversed(range(gains.shape[0])):
        cotangent, normed, pre_grad, hidden, out_grad = layer_backward(
            inputs[depth_index], cotangent, gains[depth_index], ups[depth_index], downs[depth_index]
        )
        normed_list.insert(0, normed)
        pre_list.insert(0, pre_grad)
        hidden_list.insert(0, hidden)
        out_list.insert(0, out_grad)
    factors = (
        jnp.stack(normed_list),
        jnp.stack(pre_list),
        jnp.stack(hidden_list),
        jnp.stack(out_list),
    )
    return (cotangent, factors)


def compose(earlier, later):
    return (earlier[0] * later[0], later[0] * earlier[1] + later[1])


def shards(c_guess, adj_guess, norm_gain, w_up, w_down, coarse_rate):
    position = lax.axis_index("layer")
    devices = lax.axis_size("layer")
    leading = position == 0
    trailing = position == devices - 1
    start_state = c_guess[0]
    decay_rate = coarse_rate[0]
    identity_map = (jnp.ones_like(decay_rate), jnp.zeros_like(start_state))
    block_end = block_forward(start_state, norm_gain, w_up, w_down)
    forward_rate = jnp.where(leading, jnp.zeros_like(decay_rate), decay_rate)
    forward_shift = block_end - forward_rate * start_state
    _, carried = carried_in((forward_rate, forward_shift), "layer", compose, identity_map, False)
    point = jnp.where(leading, start_state, carried)
    inputs = block_inputs(point, norm_gain, w_up, w_down)
    adjoint_guess = adj_guess[0]
    begin, _ = block_backward(inputs, adjoint_guess, norm_gain, w_up, w_down)
    backward_rate = jnp.where(trailing, jnp.zeros_like(decay_rate), decay_rate)
    backward_shift = begin - backward_rate * adjoint_guess
    _, carried_back = carried_in(
        (backward_rate, backward_shift), "layer", compose, identity_map, True
    )
    adjoint = jnp.where(trailing, adjoint_guess, carried_back)
    _, factors = block_backward(inputs, adjoint, norm_gain, w_up, w_down)
    normed_all, pre_all, hidden_all, out_all = factors
    group = lax.axis_size("dp")
    member = lax.axis_index("dp")
    width_share = w_up.shape[1] // group
    hidden_share = w_up.shape[2] // group
    piece_normed = lax.all_gather(normed_all, "dp", axis=1, tiled=True)
    piece_pre = lax.all_gather(pre_all, "dp", axis=1, tiled=True)
    piece_hidden = lax.all_gather(hidden_all, "dp", axis=1, tiled=True)
    piece_out = lax.all_gather(out_all, "dp", axis=1, tiled=True)
    normed_cols = lax.dynamic_slice_in_dim(piece_normed, member * width_share, width_share, 2)
    hidden_cols = lax.dynamic_slice_in_dim(piece_hidden, member * hidden_share, hidden_share, 2)
    up_part = jnp.einsum("ltd,ltf->ldf", normed_cols, piece_pre, preferred_element_type=jnp.float32)
    down_part = jnp.einsum(
        "ltf,ltd->lfd", hidden_cols, piece_out, preferred_element_type=jnp.float32
    )
    return (point[None], adjoint[None], up_part, down_part)


def solution(mesh):
    return jax.shard_map(
        shards,
        mesh=mesh,
        in_specs=(
            P("layer", "dp", None),
            P("layer", "dp", None),
            P("layer", None),
            P("layer", None, None),
            P("layer", None, None),
            P("layer", None),
        ),
        out_specs=(
            P("layer", "dp", None),
            P("layer", "dp", None),
            P("layer", "dp", None),
            P("layer", "dp", None),
        ),
        check_vma=False,
    )
```

profile of v0, /device:TPU:0, one launch (start us, length us, event | category | flops | bytes accessed | tf_op | source)
XLA Modules:
  0.0 239.0 jit_solution(10892800529612794329)
XLA Ops:
  9.1 3.2 %multiply_reduce_fusion.5 = (f32[128]{0:T(128)S(1)}, f32[128,512]{1,0:T(8,128)S(1)}) fusion(bf16[2,2048,512]{2,1,0:T(8,128)(2,1)} %param.14, bf16[2,512,2048]{2,1,0:T(8,128)(2,1)} %param.13, f32[1,128,512]{2,1,0:T(8,128)} %param.10, f32[512]{0:T(512)S(1)} %bitcast.178, f32[128]{0:T(128)S(1)} %add_rsqrt_fusion.3), kind=kOutput, calls=%fused_computation.108 | convolution fusion | flops 538640256 | bytes 4983808 | tf_op jit(solution)/shard_map/dot_general | solution.py:36
  12.3 3.7 %fusion.76 = f32[128,512]{1,0:T(8,128)} fusion(f32[128,512]{1,0:T(8,128)S(1)} %get-tuple-element.301, bf16[2,2048,512]{2,1,0:T(8,128)(2,1)} %param.14, bf16[2,512,2048]{2,1,0:T(8,128)(2,1)} %param.13, f32[1,128,512]{2,1,0:T(8,128)S(1)} %copy-done.3, f32[512]{0:T(512)S(1)} %bitcast.184, f32[512]{0:T(512)S(1)} %bitcast.173, f32[128]{0:T(128)S(1)} %add_rsqrt_fusion.2), kind=kOutput, calls=%fused_computation.66 | convolution fusion | flops 538640384 | bytes 5247488 | tf_op jit(solution)/shard_map/dot_general | solution.py:36
  16.1 23.3 %all-gather.2 = f32[16,1,512]{2,1,0:T(1,128)S(1)} all-gather(f32[1,1,512]{2,1,0:T(1,128)S(1)} %bitcast.185), channel_id=1, replica_groups=mesh['layer'=16,'dp'=2] {'layer'}, dimensions={0}, use_global_device_ids=true | all-gather | bytes 34816 | tf_op jit(solution)/shard_map/all_gather | solution.py:12
  39.4 29.9 %all-gather.13.cloned.1.call-done = f32[2048,512]{1,0:T(8,128)} async-done(((f32[128,512]{1,0:T(8,128)}), f32[2048,512]{1,0:T(8,128)}) %all-gather.13.cloned.1.call-update) | async-done | bytes 4194320 | tf_op jit(solution)/shard_map/all_gather | solution.py:12
  69.3 19.1 %while.30 = (s32[]{:T(128)}, f32[128,512]{1,0:T(8,128)S(1)}, s32[]{:T(128)}, f32[16,512]{1,0:T(8,128)S(1)}, f32[16,128,512]{2,1,0:T(8,128)}, /*index=5*/s32[]{:T(128)}, s32[]{:T(128)}) while((s32[]{:T(128)}, f32[128,512]{1,0:T(8,128)S(1)}, s32[]{:T(128)}, f32[16,512]{1,0:T(8,128)S(1)}, f32[16,128,512]{2,1,0:T(8,128)}, ...), condition=%wide.region_3.4_spmd.clone, body=%wide.region_2.3_spmd.clone.sunk | while | flops 262148 | bytes 792689 | solution.py:23
  70.5 1.2 fusion.150
  88.6 2.2 fusion.31
  92.0 1.5 copy-done.1
  94.1 4.5 %multiply_reduce_fusion.2 = (f32[128]{0:T(128)S(1)}, f32[128,512]{1,0:T(8,128)}) fusion(f32[128,512]{1,0:T(8,128)S(1)} %get-tuple-element.303, f32[128]{0:T(128)S(1)} %add_rsqrt_fusion, f32[512]{0:T(512)S(1)} %bitcast.175, bf16[2,512,2048]{2,1,0:T(8,128)(2,1)} %param.13, bf16[2,2048,512]{2,1,0:T(8,128)(2,1)} %param.14, f32[128,2048]{1,0:T(8,128)S(1)} %fusion.19, ...), kind=kOutput, calls=%fused_computation.101 | convolution fusion | flops 539623296 | bytes 6032384 | tf_op jit(solution)/shard_map/dot_general | solution.py:50
  98.6 3.9 %fusion.49 = f32[128,512]{1,0:T(8,128)S(1)} fusion(bf16[2,512,2048]{2,1,0:T(8,128)(2,1)} %param.13, bf16[2,2048,512]{2,1,0:T(8,128)(2,1)} %param.14, f32[128,2048]{1,0:T(8,128)S(1)} %fusion.31, f32[512]{0:T(512)S(1)} %bitcast.180, f32[1,128,512]{2,1,0:T(8,128)S(1)} %copy-done.4, f32[128,512]{1,0:T(8,128)} %get-tuple-element.305, ...), kind=kOutput, calls=%fused_computation.57 | convolution fusion | flops 539754496 | bytes 6294528 | tf_op jit(solution)/shard_map/dot_general | solution.py:50
  102.7 1.8 fusion.133
  104.6 19.1 %all-gather.3 = f32[16,1,512]{2,1,0:T(1,128)S(1)} all-gather(f32[1,1,512]{2,1,0:T(1,128)S(1)} %bitcast.183), channel_id=1, replica_groups=mesh['layer'=16,'dp'=2] {'layer'}, dimensions={0}, use_global_device_ids=true | all-gather | bytes 34816 | tf_op jit(solution)/shard_map/all_gather | solution.py:12
  125.4 28.2 %all-gather.15.cloned.1.call-done = f32[2048,512]{1,0:T(8,128)} async-done(((f32[128,512]{1,0:T(8,128)}), f32[2048,512]{1,0:T(8,128)}) %all-gather.15.cloned.1.call-update) | async-done | bytes 4194320 | tf_op jit(solution)/shard_map/all_gather | solution.py:12
  153.7 19.3 %while.31 = (s32[]{:T(128)}, f32[128,512]{1,0:T(8,128)S(1)}, s32[]{:T(128)}, f32[16,512]{1,0:T(8,128)S(1)}, f32[16,128,512]{2,1,0:T(8,128)}, /*index=5*/s32[]{:T(128)}, s32[]{:T(128)}, s32[]{:T(128)}, s32[]{:T(128)}) while((s32[]{:T(128)}, f32[128,512]{1,0:T(8,128)S(1)}, s32[]{:T(128)}, f32[16,512]{1,0:T(8,128)S(1)}, ...), condition=%wide.region_9.10_spmd.clone, body=%wide.region_8.9_spmd.clone.sunk | while | flops 262152 | bytes 792751 | solution.py:23
  159.7 1.2 fusion.151
  160.9 1.2 fusion.151
  162.1 1.2 fusion.151
  163.3 1.2 fusion.151
  173.0 2.6 %fusion.8 = bf16[128,2048]{1,0:T(8,128)(2,1)S(1)} fusion(bf16[2,2048,512]{2,1,0:T(8,128)(2,1)} %param.14, f32[128,2048]{1,0:T(8,128)S(1)} %fusion.19, f32[128,512]{1,0:T(8,128)S(1)} %get-tuple-element.289), kind=kOutput, calls=%fused_computation.16 | convolution fusion | flops 270925824 | bytes 3932160 | tf_op jit(solution)/shard_map/dot_general | solution.py:46
  180.2 12.6 %all_gather.38 = bf16[2,256,512]{2,1,0:T(8,128)(2,1)S(1)} all-gather(bf16[2,128,512]{2,1,0:T(8,128)(2,1)S(1)} %pad_maximum_fusion.2), channel_id=1, replica_groups=mesh['layer'=16,'dp'=2] {'dp'}, dimensions={1}, use_global_device_ids=true | all-gather | bytes 786432 | tf_op jit(solution)/shard_map/all_gather | solution.py:121
  192.8 8.8 %all_gather.41 = bf16[2,256,512]{2,1,0:T(8,128)(2,1)S(1)} all-gather(bf16[2,128,512]{2,1,0:T(8,128)(2,1)S(1)} %pad_maximum_fusion.3), channel_id=1, replica_groups=mesh['layer'=16,'dp'=2] {'dp'}, dimensions={1}, use_global_device_ids=true | all-gather | bytes 786432 | tf_op jit(solution)/shard_map/all_gather | solution.py:124
  201.6 4.1 %fusion.79 = f32[2,1024,512]{2,1,0:T(8,128)} fusion(bf16[2,256,512]{2,1,0:T(8,128)(2,1)S(1)} %all_gather.41, bf16[2,256,2048]{2,1,0:T(8,128)(2,1)} %all-gather.11.cloned.1.call-done, s32[]{:T(128)S(6)} %select_n.96), kind=kOutput, calls=%fused_computation.69 | convolution fusion | flops 536870912 | bytes 5767172 | tf_op jit(solution)/shard_map/ltf,ltd->lfd/dot_general | solution.py:128
  205.7 22.4 %all-gather.9.cloned.1.call-done = bf16[2,256,2048]{2,1,0:T(8,128)(2,1)} async-done(((bf16[2,128,2048]{2,1,0:T(8,128)(2,1)}), bf16[2,256,2048]{2,1,0:T(8,128)(2,1)}) %all-gather.9.cloned.1.call-update) | async-done | bytes 2097168 | tf_op jit(solution)/shard_map/all_gather | solution.py:122
  228.1 4.4 %fusion.100 = f32[2,256,2048]{2,1,0:T(8,128)} fusion(bf16[2,256,2048]{2,1,0:T(8,128)(2,1)} %all-gather.9.cloned.1.call-done, bf16[2,256,512]{2,1,0:T(8,128)(2,1)S(1)} %all_gather.38, s32[]{:T(128)S(6)} %select_n.95), kind=kOutput, calls=%fused_computation.97 | convolution fusion | flops 536870912 | bytes 6553604 | tf_op jit(solution)/shard_map/ltd,ltf->ldf/dot_general | solution.py:127
  (112 shorter events, 41.8 us)
Async XLA Ops:
  7.2 62.2 %all-gather.13.cloned.1.call-start = ((), (), s32[]{:S(2)}) async-start(), calls=%async_computation.2 | async-start | bytes 4456448 | tf_op jit(solution)/shard_map/all_gather | solution.py:12
  9.1 3.2 %copy-start.6 = (f32[1,512]{1,0:T(1,128)S(1)}, f32[1,512]{1,0:T(1,128)}, u32[]{:S(2)}) copy-start(f32[1,512]{1,0:T(1,128)} %param.15) | copy-start | bytes 6148
  9.1 3.2 %copy-start.3 = (f32[1,128,512]{2,1,0:T(8,128)S(1)}, f32[1,128,512]{2,1,0:T(8,128)}, u32[]{:S(2)}) copy-start(f32[1,128,512]{2,1,0:T(8,128)} %param.10) | copy-start | bytes 786436
  16.1 137.6 %all-gather.15.cloned.1.call-start = ((), (), s32[]{:S(2)}) async-start(), calls=%async_computation.3 | async-start | bytes 4456448 | tf_op jit(solution)/shard_map/all_gather | solution.py:12
  88.5 2.9 %copy-start.7 = (bf16[2,2048,512]{2,1,0:T(8,128)(2,1)S(1)}, bf16[2,2048,512]{2,1,0:T(8,128)(2,1)}, u32[]{:S(2)}) copy-start(bf16[2,2048,512]{2,1,0:T(8,128)(2,1)} %param.14) | copy-start | bytes 12582916
  88.6 14.0 %copy-start = (f32[128,512]{1,0:T(8,128)}, f32[128,512]{1,0:T(8,128)S(1)}, u32[]{:S(2)}) copy-start(f32[128,512]{1,0:T(8,128)S(1)} %get-tuple-element.291) | copy-start | bytes 786436
  91.4 2.2 copy-start.1
  91.4 2.7 %copy-start.4 = (f32[1,128,512]{2,1,0:T(8,128)S(1)}, f32[1,128,512]{2,1,0:T(8,128)}, u32[]{:S(2)}) copy-start(f32[1,128,512]{2,1,0:T(8,128)} %param.11) | copy-start | bytes 786436
  104.5 97.1 %all-gather.11.cloned.1.call-start = ((), (), s32[]{:S(2)}) async-start(), calls=%async_computation.1 | async-start | bytes 3145728 | tf_op jit(solution)/shard_map/all_gather | solution.py:123
  125.4 102.8 %all-gather.9.cloned.1.call-start = ((), (), s32[]{:S(2)}) async-start(), calls=%async_computation | async-start | bytes 3145728 | tf_op jit(solution)/shard_map/all_gather | solution.py:122
  173.0 3.9 %copy-start.5 = (f32[128,512]{1,0:T(8,128)}, f32[128,512]{1,0:T(8,128)S(1)}, u32[]{:S(2)}) copy-start(f32[128,512]{1,0:T(8,128)S(1)} %get-tuple-element.289) | copy-start | bytes 786436
  173.0 2.9 %copy-start.2 = (bf16[2,512,2048]{2,1,0:T(8,128)(2,1)S(1)}, bf16[2,512,2048]{2,1,0:T(8,128)(2,1)}, u32[]{:S(2)}) copy-start(bf16[2,512,2048]{2,1,0:T(8,128)(2,1)} %param.13) | copy-start | bytes 12582916
  175.9 2.2 copy-start.8
Sparse Core Ops, SparseCore 0:
  16.2 53.0 all-gather.12
  104.6 48.9 all-gather.14
  155.8 35.1 all-gather.10
  192.9 35.1 all-gather.8
where the time goes:
time: 240 us; the launch traced here: 239 us
  waiting for transfers between devices  80.6 us (34%)
  blocking collectives  63.9 us (27%)
  other arithmetic  43.3 us (18%)
  matrix products  31.5 us (13%)
  between operations  14 us (6%)
  local copies, waits for them, and re-layouts  4.58 us (2%)
    all_gather x2, waiting for transfers between devices, carried_in(): everything = jax.tree.map(lambda part: lax.all_gather(part, axis), x)  58.1 us
    all_gather x2, blocking collectives, carried_in(): everything = jax.tree.map(lambda part: lax.all_gather(part, axis), x)  42.4 us
    select_n x32, other arithmetic, step(): return jax.tree.map(lambda a, b: jnp.where(reached, a, b), new, before)  37.1 us
    all_gather x1, waiting for transfers between devices, shards(): piece_pre = lax.all_gather(pre_all, 'dp', axis=1, tiled=True)  22.4 us
    all_gather x1, blocking collectives, shards(): piece_normed = lax.all_gather(normed_all, 'dp', axis=1, tiled=True)  12.6 us
    dot_general x3, matrix products, layer_backward(): jnp.dot(pre_grad, up_matrix.T, preferred_element_type=jnp.float32)  9.26 us
    all_gather x1, blocking collectives, shards(): piece_out = lax.all_gather(out_all, 'dp', axis=1, tiled=True)  8.79 us
    dot_general x3, matrix products, layer_forward(): jnp.dot(hidden, down_matrix, preferred_element_type=jnp.float32)  7.55 us
  transfers between devices with their start and end apart: 4, of which 3 were waited for; matrix products, arithmetic and copies ran while one was open for 13% of the time, Pallas kernels for 0%

commit v1 on v0

--- a/solution.py
+++ b/solution.py
@@ -119,7 +119,7 @@
     width_share = w_up.shape[1] // group
     hidden_share = w_up.shape[2] // group
     piece_normed = lax.all_gather(normed_all, "dp", axis=1, tiled=True)
-    piece_pre = lax.all_gather(pre_all, "dp", axis=1, tiled=True)
+    piece_pre = jnp.concatenate(lax.all_gather(pre_all, "dp"), axis=1)
     piece_hidden = lax.all_gather(hidden_all, "dp", axis=1, tiled=True)
     piece_out = lax.all_gather(out_all, "dp", axis=1, tiled=True)
     normed_cols = lax.dynamic_slice_in_dim(piece_normed, member * width_share, width_share, 2)

time: 240 us -> 241 us (level)
  local copies, waits for them, and re-layouts: 4.58 us -> 7.01 us
where the time goes in v1:
time: 241 us; the launch traced here: 239 us
  waiting for transfers between devices  80.6 us (33%)
  blocking collectives  63.8 us (26%)
  other arithmetic  43.3 us (18%)
  matrix products  29.2 us (12%)
  between operations  14 us (6%)
  local copies, waits for them, and re-layouts  7.01 us (3%)
    all_gather x2, waiting for transfers between devices, carried_in(): everything = jax.tree.map(lambda part: lax.all_gather(part, axis), x)  58.1 us
    all_gather x2, blocking collectives, carried_in(): everything = jax.tree.map(lambda part: lax.all_gather(part, axis), x)  42.4 us
    select_n x32, other arithmetic, step(): return jax.tree.map(lambda a, b: jnp.where(reached, a, b), new, before)  37.1 us
    all_gather x1, waiting for transfers between devices, shards(): piece_pre = jnp.concatenate(lax.all_gather(pre_all, 'dp'), axis=1)  22.4 us
    all_gather x1, blocking collectives, shards(): piece_normed = lax.all_gather(normed_all, 'dp', axis=1, tiled=True)  12.6 us
    all_gather x1, blocking collectives, shards(): piece_out = lax.all_gather(out_all, 'dp', axis=1, tiled=True)  8.79 us
    dot_general x3, matrix products, layer_backward(): jnp.dot(pre_grad, up_matrix.T, preferred_element_type=jnp.float32)  8.56 us
    dot_general x3, matrix products, layer_forward(): jnp.dot(hidden, down_matrix, preferred_element_type=jnp.float32)  7.56 us
  transfers between devices with their start and end apart: 4, of which 3 were waited for; matrix products, arithmetic and copies ran while one was open for 13% of the time, Pallas kernels for 0%

profile of v1, /device:TPU:0, one launch (start us, length us, event | category | flops | bytes accessed | tf_op | source)
XLA Modules:
  0.0 239.2 jit_solution(5272726084246386224)
XLA Ops:
  9.1 3.2 %multiply_reduce_fusion.5 = (f32[128]{0:T(128)S(1)}, f32[128,512]{1,0:T(8,128)S(1)}) fusion(bf16[2,2048,512]{2,1,0:T(8,128)(2,1)} %param.14, bf16[2,512,2048]{2,1,0:T(8,128)(2,1)} %param.13, f32[1,128,512]{2,1,0:T(8,128)} %param.10, f32[512]{0:T(512)S(1)} %bitcast.184, f32[128]{0:T(128)S(1)} %add_rsqrt_fusion.3), kind=kOutput, calls=%fused_computation.108 | convolution fusion | flops 538640256 | bytes 4983808 | tf_op jit(solution)/shard_map/dot_general | solution.py:36
  12.3 3.7 %fusion.76 = f32[128,512]{1,0:T(8,128)} fusion(f32[128,512]{1,0:T(8,128)S(1)} %get-tuple-element.301, bf16[2,2048,512]{2,1,0:T(8,128)(2,1)} %param.14, bf16[2,512,2048]{2,1,0:T(8,128)(2,1)} %param.13, f32[1,128,512]{2,1,0:T(8,128)S(1)} %copy-done.3, f32[512]{0:T(512)S(1)} %bitcast.190, f32[512]{0:T(512)S(1)} %bitcast.179, f32[128]{0:T(128)S(1)} %add_rsqrt_fusion.2), kind=kOutput, calls=%fused_computation.66 | convolution fusion | flops 538640384 | bytes 5247488 | tf_op jit(solution)/shard_map/dot_general | solution.py:36
  16.1 23.3 %all-gather.3 = f32[16,1,512]{2,1,0:T(1,128)S(1)} all-gather(f32[1,1,512]{2,1,0:T(1,128)S(1)} %bitcast.191), channel_id=1, replica_groups=mesh['layer'=16,'dp'=2] {'layer'}, dimensions={0}, use_global_device_ids=true | all-gather | bytes 34816 | tf_op jit(solution)/shard_map/all_gather | solution.py:12
  39.5 29.9 %all-gather.12.cloned.1.call-done = f32[2048,512]{1,0:T(8,128)} async-done(((f32[128,512]{1,0:T(8,128)}), f32[2048,512]{1,0:T(8,128)}) %all-gather.12.cloned.1.call-update) | async-done | bytes 4194320 | tf_op jit(solution)/shard_map/all_gather | solution.py:12
  69.3 19.1 %while.30 = (s32[]{:T(128)}, f32[128,512]{1,0:T(8,128)S(1)}, s32[]{:T(128)}, f32[16,512]{1,0:T(8,128)S(1)}, f32[16,128,512]{2,1,0:T(8,128)}, /*index=5*/s32[]{:T(128)}, s32[]{:T(128)}) while((s32[]{:T(128)}, f32[128,512]{1,0:T(8,128)S(1)}, s32[]{:T(128)}, f32[16,512]{1,0:T(8,128)S(1)}, f32[16,128,512]{2,1,0:T(8,128)}, ...), condition=%wide.region_3.4_spmd.clone, body=%wide.region_2.3_spmd.clone.sunk | while | flops 262148 | bytes 792689 | solution.py:23
  88.6 2.3 fusion.31
  92.0 1.5 copy-done.1
  94.1 3.9 %multiply_reduce_fusion.2 = (f32[128]{0:T(128)S(1)}, f32[128,512]{1,0:T(8,128)S(1)}) fusion(f32[128,512]{1,0:T(8,128)S(1)} %get-tuple-element.303, f32[128]{0:T(128)S(1)} %add_rsqrt_fusion, f32[512]{0:T(512)S(1)} %bitcast.181, bf16[2,512,2048]{2,1,0:T(8,128)(2,1)} %param.13, bf16[2,2048,512]{2,1,0:T(8,128)(2,1)} %param.14, f32[128,2048]{1,0:T(8,128)S(1)} %fusion.19, ...), kind=kOutput, calls=%fused_computation.101 | convolution fusion | flops 539623296 | bytes 6032384 | tf_op jit(solution)/shard_map/dot_general | solution.py:50
  98.6 3.8 %fusion.49 = f32[128,512]{1,0:T(8,128)S(1)} fusion(bf16[2,512,2048]{2,1,0:T(8,128)(2,1)} %param.13, bf16[2,2048,512]{2,1,0:T(8,128)(2,1)} %param.14, f32[128,2048]{1,0:T(8,128)S(1)} %fusion.31, f32[512]{0:T(512)S(1)} %bitcast.186, f32[1,128,512]{2,1,0:T(8,128)S(1)} %copy-done.4, f32[128,512]{1,0:T(8,128)S(1)} %get-tuple-element.305, ...), kind=kOutput, calls=%fused_computation.57 | convolution fusion | flops 539754496 | bytes 6294528 | tf_op jit(solution)/shard_map/dot_general | solution.py:50
  102.7 1.8 fusion.133
  104.6 19.1 %all-gather.4 = f32[16,1,512]{2,1,0:T(1,128)S(1)} all-gather(f32[1,1,512]{2,1,0:T(1,128)S(1)} %bitcast.189), channel_id=1, replica_groups=mesh['layer'=16,'dp'=2] {'layer'}, dimensions={0}, use_global_device_ids=true | all-gather | bytes 34816 | tf_op jit(solution)/shard_map/all_gather | solution.py:12
  125.4 28.3 %all-gather.14.cloned.1.call-done = f32[2048,512]{1,0:T(8,128)} async-done(((f32[128,512]{1,0:T(8,128)}), f32[2048,512]{1,0:T(8,128)}) %all-gather.14.cloned.1.call-update) | async-done | bytes 4194320 | tf_op jit(solution)/shard_map/all_gather | solution.py:12
  153.7 19.3 %while.31 = (s32[]{:T(128)}, f32[128,512]{1,0:T(8,128)S(1)}, s32[]{:T(128)}, f32[16,512]{1,0:T(8,128)S(1)}, f32[16,128,512]{2,1,0:T(8,128)}, /*index=5*/s32[]{:T(128)}, s32[]{:T(128)}, s32[]{:T(128)}, s32[]{:T(128)}) while((s32[]{:T(128)}, f32[128,512]{1,0:T(8,128)S(1)}, s32[]{:T(128)}, f32[16,512]{1,0:T(8,128)S(1)}, ...), condition=%wide.region_9.10_spmd.clone, body=%wide.region_8.9_spmd.clone.sunk | while | flops 262152 | bytes 792751 | solution.py:23
  159.7 1.2 fusion.151
  160.9 1.2 fusion.151
  162.2 1.2 fusion.151
  163.4 1.2 fusion.151
  173.1 2.6 %fusion.8 = bf16[128,2048]{1,0:T(8,128)(2,1)S(1)} fusion(bf16[2,2048,512]{2,1,0:T(8,128)(2,1)} %param.14, f32[128,2048]{1,0:T(8,128)S(1)} %fusion.19, f32[128,512]{1,0:T(8,128)S(1)} %get-tuple-element.289), kind=kOutput, calls=%fused_computation.16 | convolution fusion | flops 270925824 | bytes 3932160 | tf_op jit(solution)/shard_map/dot_general | solution.py:46
  180.2 12.6 %all_gather.41 = bf16[2,256,512]{2,1,0:T(8,128)(2,1)S(1)} all-gather(bf16[2,128,512]{2,1,0:T(8,128)(2,1)S(1)} %pad_maximum_fusion.2), channel_id=1, replica_groups=mesh['layer'=16,'dp'=2] {'dp'}, dimensions={1}, use_global_device_ids=true | all-gather | bytes 786432 | tf_op jit(solution)/shard_map/all_gather | solution.py:121
  192.8 8.8 %all_gather.45 = bf16[2,256,512]{2,1,0:T(8,128)(2,1)S(1)} all-gather(bf16[2,128,512]{2,1,0:T(8,128)(2,1)S(1)} %pad_maximum_fusion.3), channel_id=1, replica_groups=mesh['layer'=16,'dp'=2] {'dp'}, dimensions={1}, use_global_device_ids=true | all-gather | bytes 786432 | tf_op jit(solution)/shard_map/all_gather | solution.py:124
  201.6 4.1 %fusion.79 = f32[2,1024,512]{2,1,0:T(8,128)} fusion(bf16[2,256,512]{2,1,0:T(8,128)(2,1)S(1)} %all_gather.45, bf16[2,256,2048]{2,1,0:T(8,128)(2,1)} %all-gather.10.cloned.1.call-done, s32[]{:T(128)S(6)} %select_n.96), kind=kOutput, calls=%fused_computation.69 | convolution fusion | flops 536870912 | bytes 5767172 | tf_op jit(solution)/shard_map/ltf,ltd->lfd/dot_general | solution.py:128
  205.8 22.4 %all-gather.16.cloned.1.call-done = bf16[4,128,2048]{2,1,0:T(8,128)(2,1)} async-done(((bf16[2,128,2048]{2,1,0:T(8,128)(2,1)}), bf16[4,128,2048]{2,1,0:T(8,128)(2,1)}) %all-gather.16.cloned.1.call-update) | async-done | bytes 2097168 | tf_op jit(solution)/shard_map/all_gather | solution.py:122
  228.2 1.7 copy.13
  229.9 2.8 %fusion.100 = f32[2,256,2048]{2,1,0:T(8,128)} fusion(bf16[2,256,2048]{2,1,0:T(8,128)(2,1)S(1)} %bitcast.167, bf16[2,256,512]{2,1,0:T(8,128)(2,1)S(1)} %all_gather.41, s32[]{:T(128)S(6)} %select_n.95), kind=kOutput, calls=%fused_computation.97 | convolution fusion | flops 536870912 | bytes 6553604 | tf_op jit(solution)/shard_map/ltd,ltf->ldf/dot_general | solution.py:127
  (115 shorter events, 43.6 us)
Async XLA Ops:
  7.2 62.2 %all-gather.12.cloned.1.call-start = ((), (), s32[]{:S(2)}) async-start(), calls=%async_computation.1 | async-start | bytes 4456448 | tf_op jit(solution)/shard_map/all_gather | solution.py:12
  9.1 3.2 %copy-start.7 = (f32[1,512]{1,0:T(1,128)S(1)}, f32[1,512]{1,0:T(1,128)}, u32[]{:S(2)}) copy-start(f32[1,512]{1,0:T(1,128)} %param.15) | copy-start | bytes 6148
  9.1 3.2 %copy-start.3 = (f32[1,128,512]{2,1,0:T(8,128)S(1)}, f32[1,128,512]{2,1,0:T(8,128)}, u32[]{:S(2)}) copy-start(f32[1,128,512]{2,1,0:T(8,128)} %param.10) | copy-start | bytes 786436
  16.1 137.6 %all-gather.14.cloned.1.call-start = ((), (), s32[]{:S(2)}) async-start(), calls=%async_computation.2 | async-start | bytes 4456448 | tf_op jit(solution)/shard_map/all_gather | solution.py:12
  88.5 2.9 %copy-start.8 = (bf16[2,2048,512]{2,1,0:T(8,128)(2,1)S(1)}, bf16[2,2048,512]{2,1,0:T(8,128)(2,1)}, u32[]{:S(2)}) copy-start(bf16[2,2048,512]{2,1,0:T(8,128)(2,1)} %param.14) | copy-start | bytes 12582916
  88.6 14.0 %copy-start = (f32[128,512]{1,0:T(8,128)}, f32[128,512]{1,0:T(8,128)S(1)}, u32[]{:S(2)}) copy-start(f32[128,512]{1,0:T(8,128)S(1)} %get-tuple-element.291) | copy-start | bytes 786436
  91.4 2.2 copy-start.1
  91.4 2.7 %copy-start.4 = (f32[1,128,512]{2,1,0:T(8,128)S(1)}, f32[1,128,512]{2,1,0:T(8,128)}, u32[]{:S(2)}) copy-start(f32[1,128,512]{2,1,0:T(8,128)} %param.11) | copy-start | bytes 786436
  97.9 0.7 copy-start.6
  104.5 97.1 %all-gather.10.cloned.1.call-start = ((), (), s32[]{:S(2)}) async-start(), calls=%async_computation | async-start | bytes 3145728 | tf_op jit(solution)/shard_map/all_gather | solution.py:123
  125.4 102.8 %all-gather.16.cloned.1.call-start = ((), (), s32[]{:S(2)}) async-start(), calls=%async_computation.3 | async-start | bytes 3145728 | tf_op jit(solution)/shard_map/all_gather | solution.py:122
  173.0 3.9 %copy-start.5 = (f32[128,512]{1,0:T(8,128)}, f32[128,512]{1,0:T(8,128)S(1)}, u32[]{:S(2)}) copy-start(f32[128,512]{1,0:T(8,128)S(1)} %get-tuple-element.289) | copy-start | bytes 786436
  173.1 2.9 %copy-start.2 = (bf16[2,512,2048]{2,1,0:T(8,128)(2,1)S(1)}, bf16[2,512,2048]{2,1,0:T(8,128)(2,1)}, u32[]{:S(2)}) copy-start(bf16[2,512,2048]{2,1,0:T(8,128)(2,1)} %param.13) | copy-start | bytes 12582916
  176.0 2.2 copy-start.9
Sparse Core Ops, SparseCore 0:
  16.2 53.0 all-gather.11
  104.6 48.9 all-gather.13
  155.8 35.0 all-gather.9
  192.9 35.2 all-gather.15
